TPU v7x, 32 devices: a whole 2x2x4 slice. The times are simulated.
32 devices in a mesh: grp: 2 (over x), wide: 16 (over z, y, core).
Axes of the slice: x: 2, y: 2, z: 4, core: 2. Of those that a mesh axis runs over, the one named last changes fastest.
Arguments:
- raw: bfloat16 [4096, 16, 2048], P(('grp', 'wide')), parts along dimension 0, may hold values from -6 to 6
- cell_feed: int32 [1024], replicated, may hold values from 0 to 1023, each once
- dm_delay: int32 [1024, 1024], replicated, may hold values from 0 to 15
Outputs:
- dedispersed: float32 [2048, 16, 1024], P(('grp', 'wide')), parts along dimension 0
There are 2 independent parts, one for each index of `grp`. A program takes and returns all parts, laid end to end along the dimension named above; an argument that names none is the same for every part. Nothing has to cross between parts.
Inputs may be any that keep to these rules, and one draw needn't show every extreme that they name: `cell_feed`: every antenna stands at exactly one cell.
All inputs are finite; a program needn't handle non-finite values.
Results may differ from a plain program's by a relative error of at most 0.0084.
Values may be sent and summed in bfloat16 or wider, within the bound.
No kernel may reach another device: no remote copies, remote signals or barrier semaphores. Data moves between devices by JAX's collectives and lax.ppermute only.
A program may use at most 128 MiB of HBM per device.

v0:
```python
import math
import jax
import jax.numpy as jnp
import numpy as np
from jax import lax
from jax.sharding import PartitionSpec as P

EAST_COSINE = np.array([[1, 1, 1, 1], [1, 0, -1, 0], [1, -1, 1, -1], [1, 0, -1, 0]], np.float32)
EAST_SINE = np.array([[0, 0, 0, 0], [0, 1, 0, -1], [0, 0, 0, 0], [0, -1, 0, 1]], np.float32)


def phase_pair(count, length):
    angle = (count % length).astype(jnp.float32) * (2.0 * math.pi / length)
    return (jnp.cos(angle), jnp.sin(angle))


def channel_table(samples, width):
    sample_ids = lax.broadcasted_iota(jnp.int32, (samples, width), 0)
    freq_ids = lax.broadcasted_iota(jnp.int32, (samples, width), 1)
    cosine, sine = phase_pair(sample_ids * freq_ids, samples)
    factor = 1.0 / math.sqrt(samples)
    return jnp.concatenate([cosine * factor, -sine * factor], axis=1).astype(jnp.bfloat16)


def sky_table(cells):
    rows = lax.broadcasted_iota(jnp.int32, (cells, cells), 0)
    cols = lax.broadcasted_iota(jnp.int32, (cells, cells), 1)
    cosine, sine = phase_pair(rows * cols, cells)
    real_row = jnp.stack([cosine, sine], axis=-1)
    imag_row = jnp.stack([-sine, cosine], axis=-1)
    factor = 1.0 / math.sqrt(cells)
    return (jnp.stack([real_row, imag_row], axis=1) * factor).astype(jnp.bfloat16)


def transform_table(frames):
    terms = frames // 2 + 1
    harmonic = lax.broadcasted_iota(jnp.int32, (terms, frames), 0)
    moment = lax.broadcasted_iota(jnp.int32, (terms, frames), 1)
    cosine, sine = phase_pair(harmonic * moment, frames)
    return jnp.stack([cosine, -sine]).astype(jnp.bfloat16)


def beam_power(spec, feed_index, table):
    grid = jnp.take(spec, feed_index.reshape(-1), axis=0)
    grid = grid.reshape(feed_index.shape + spec.shape[1:])
    beams = jnp.einsum("joni,penrif->poerfj", table, grid, preferred_element_type=jnp.float32)
    real_part = beams[:, 0]
    imag_part = beams[:, 1]
    cosines = jnp.asarray(EAST_COSINE)
    sines = jnp.asarray(EAST_SINE)
    high = lax.Precision.HIGHEST
    east_real = 0.5 * (
        jnp.einsum("qe,perfj->prfqj", cosines, real_part, precision=high)
        + jnp.einsum("qe,perfj->prfqj", sines, imag_part, precision=high)
    )
    east_imag = 0.5 * (
        jnp.einsum("qe,perfj->prfqj", cosines, imag_part, precision=high)
        - jnp.einsum("qe,perfj->prfqj", sines, real_part, precision=high)
    )
    power = 0.5 * jnp.sum(east_real * east_real + east_imag * east_imag, axis=0)
    return power.reshape(power.shape[0], power.shape[1], -1)


def dedisperse(spectrum, dm_delay, frames):
    base_cos, base_sin = phase_pair(jnp.transpose(dm_delay), frames)
    beams_dev = spectrum.shape[3]
    nfreq = spectrum.shape[2]

    def one_term(carry, block):
        cosine, sine = carry
        cos_half = cosine.astype(jnp.bfloat16)
        sin_half = sine.astype(jnp.bfloat16)
        upper = jnp.concatenate([cos_half, sin_half], axis=1)
        lower = jnp.concatenate([-sin_half, cos_half], axis=1)
        right = jnp.concatenate([upper, lower], axis=0)
        left = block.reshape(2 * nfreq, beams_dev)
        result = lax.dot_general(
            left, right, (((0,), (0,)), ((), ())), preferred_element_type=jnp.float32
        )
        next_cos = cosine * base_cos - sine * base_sin
        next_sin = sine * base_cos + cosine * base_sin
        return ((next_cos, next_sin), result)

    start = (jnp.ones(base_cos.shape, jnp.float32), jnp.zeros(base_cos.shape, jnp.float32))
    final, trials = lax.scan(one_term, start, spectrum)
    return trials.reshape(trials.shape[0], beams_dev, 2, -1)


def synthesis(trials, frames, nfreq):
    terms = frames // 2 + 1
    moment = lax.broadcasted_iota(jnp.int32, (frames, terms), 0)
    harmonic = lax.broadcasted_iota(jnp.int32, (frames, terms), 1)
    cosine, sine = phase_pair(moment * harmonic, frames)
    weight = jnp.where((harmonic == 0) | (harmonic * 2 == frames), 1.0, 2.0).astype(jnp.float32)
    weight = weight / (frames * math.sqrt(nfreq))
    table = jnp.stack([cosine * weight, -sine * weight], axis=1)
    return jnp.einsum("tuk,kbud->btd", table, trials, precision=lax.Precision.HIGHEST)


def body(raw, cell_feed, dm_delay):
    feed_dev, frames, samples = raw.shape
    nfreq = samples // 2
    table = channel_table(samples, nfreq)
    spectra = jnp.dot(
        raw.reshape(feed_dev * frames, samples), table, preferred_element_type=jnp.float32
    )
    spectra = spectra.astype(jnp.bfloat16).reshape(feed_dev, frames, 2, nfreq)
    cells = cell_feed.shape[0] // 4
    polar = lax.broadcasted_iota(jnp.int32, (2, 4, cells), 0)
    feed_index = 2 * cell_feed.reshape(1, 4, cells) + polar
    table_sky = sky_table(cells)
    arrived = lax.all_to_all(spectra, "wide", split_axis=3, concat_axis=0, tiled=True)
    power = beam_power(arrived, feed_index, table_sky)
    centred = (power - jnp.mean(power, axis=0, keepdims=True)).astype(jnp.bfloat16)
    time_table = transform_table(frames)
    local = jnp.einsum("okr,rfb->kofb", time_table, centred, preferred_element_type=jnp.float32)
    spectrum = lax.all_to_all(
        local.astype(jnp.bfloat16), "wide", split_axis=3, concat_axis=2, tiled=True
    )
    trials = dedisperse(spectrum, dm_delay, frames)
    return synthesis(trials, frames, nfreq)


def solution(mesh):
    placed = (P(("grp", "wide"), None, None), P(), P())
    return jax.shard_map(
        body, mesh=mesh, in_specs=placed, out_specs=P(("grp", "wide"), None, None), check_vma=False
    )
```

profile of v0, /device:TPU:13, one launch (start us, length us, event | category | flops | bytes accessed | tf_op | source)
XLA Modules:
  0.0 774.5 jit_solution(11408778004443474924)
XLA Ops:
  0.0 34.1 %multiply_convert_fusion = (bf16[2048,1024]{1,0:T(8,128)(2,1)S(1)}, bf16[2048,1024]{1,0:T(8,128)(2,1)S(1)}) fusion(), kind=kLoop, calls=%fused_computation.36 | loop fusion | flops 39845888 | bytes 8388608 | tf_op jit(solution)/shard_map/convert.3
  34.1 20.6 %convert_bitcast_fusion = bf16[2048,2048]{0,1:T(8,128)(2,1)} fusion(bf16[2048,2048]{1,0:T(8,128)(2,1)S(1)} %bitcast.101, bf16[2048,1024]{1,0:T(8,128)(2,1)S(1)} %get-tuple-element.115, bf16[2048,1024]{1,0:T(8,128)(2,1)S(1)} %get-tuple-element.116), kind=kOutput, calls=%fused_computation.35 | convolution fusion | flops 17200840704 | bytes 25165824 | tf_op jit(solution)/shard_map/dot_general | solution.py:104
  54.7 12.4 %copy.57 = bf16[2048,2048]{1,0:T(8,128)(2,1)} copy(bf16[2048,2048]{0,1:T(8,128)(2,1)} %convert_bitcast_fusion) | data formatting | bytes 16777216 | tf_op jit(solution)/shard_map/convert_element_type | solution.py:107
  67.1 14.5 %reshape.314 = bf16[128,16,2,1024]{3,2,1,0:T(2,128)(2,1)} reshape(bf16[2048,2048]{1,0:T(8,128)(2,1)} %copy.57) | data formatting | bytes 16777216 | tf_op jit(solution)/shard_map/reshape | solution.py:107
  81.6 16.8 %copy.58 = bf16[128,16,2,1024]{0,1,2,3:T(8,128)(2,1)} copy(bf16[128,16,2,1024]{3,2,1,0:T(2,128)(2,1)} %reshape.314) | data formatting | bytes 16777216 | tf_op jit(solution)/shard_map/reshape | solution.py:107
  107.7 179.9 %all-to-all-done = bf16[128,16,2,1024]{0,1,2,3:T(8,128)(2,1)} async-done(((bf16[128,16,2,1024]{0,1,2,3:T(8,128)(2,1)}), bf16[128,16,2,1024]{0,1,2,3:T(8,128)(2,1)}, u32[]{:S(2)}, u32[]{:S(2)}) %all-to-all-start) | async-done | bytes 8388640 | tf_op jit(solution)/shard_map/all_to_all | solution.py:112
  287.6 29.0 %copy.82 = bf16[16,128,16,2,64]{4,2,3,1,0:T(8,128)(2,1)} copy(bf16[16,128,16,2,64]{1,2,3,4,0:T(8,128)(2,1)} %bitcast.5) | data formatting | bytes 16777216 | tf_op jit(solution)/shard_map/all_to_all | solution.py:112
  316.7 25.0 %gather_fusion = bf16[2048,16,2,64]{3,1,2,0:T(8,128)(2,1)} fusion(bf16[2048,16,2,64]{3,1,2,0:T(8,128)(2,1)} %bitcast.92, s32[2048]{0:T(1024)S(1)} %broadcast_clamp_fusion), kind=kCustom, calls=%fused_computation | custom fusion | bytes 16785408 | tf_op jit(solution)/shard_map/jit(_take)/gather | solution.py:44
  341.7 19.8 %copy.83 = bf16[2,4,256,16,2,64]{2,1,0,5,4,3:T(4,128)(2,1)} copy(bf16[2,4,256,16,2,64]{5,3,4,2,1,0:T(8,128)(2,1)} %bitcast.93) | data formatting | bytes 16777216 | tf_op jit(solution)/shard_map/jit(_take)/gather | solution.py:44
  382.0 18.8 %fusion.31 = f32[2,16,64,256,4]{3,4,2,1,0:T(4,128)} fusion(f32[4,4,1,1,1]{1,0,4,3,2:T(4,128)S(1)} %copy-done.3, f32[2,4,16,64,256]{4,3,2,1,0:T(8,128)S(1)} %get-tuple-element.108), kind=kOutput, calls=%fused_computation.41 | convolution fusion | flops 100663296 | bytes 16777280 | tf_op jit(solution)/shard_map/qe,perfj->prfqj/dot_general | solution.py:57
  400.8 18.4 %fusion.33 = f32[2,16,64,256,4]{3,4,2,1,0:T(4,128)} fusion(f32[4,4,1,1,1]{1,0,4,3,2:T(4,128)S(1)} %copy-done.4, f32[2,4,16,64,256]{4,3,2,1,0:T(8,128)S(1)} %get-tuple-element.108), kind=kOutput, calls=%fused_computation.43 | convolution fusion | flops 100663296 | bytes 16777280 | tf_op jit(solution)/shard_map/qe,perfj->prfqj/dot_general | solution.py:54
  419.2 18.5 %fusion.35 = f32[2,16,64,256,4]{3,4,2,1,0:T(4,128)} fusion(f32[4,4,1,1,1]{1,0,4,3,2:T(4,128)S(1)} %copy-done.4, f32[2,4,16,64,256]{4,3,2,1,0:T(8,128)S(1)} %get-tuple-element.107), kind=kOutput, calls=%fused_computation.45 | convolution fusion | flops 100663296 | bytes 16777280 | tf_op jit(solution)/shard_map/qe,perfj->prfqj/dot_general | solution.py:58
  437.7 32.8 %add_reduce_fusion = f32[16,64,256,4]{2,3,1,0:T(4,128)} fusion(f32[2,16,64,256,4]{3,4,2,1,0:T(4,128)} %fusion.31, f32[2,16,64,256,4]{3,4,2,1,0:T(4,128)} %fusion.35, f32[2,16,64,256,4]{3,4,2,1,0:T(4,128)} %fusion.33, f32[4,4,1,1,1]{1,0,4,3,2:T(4,128)S(1)} %copy-done.3, f32[2,4,16,64,256]{4,3,2,1,0:T(8,128)} %copy-done.1), kind=kOutput, calls=%fused_computation.33 | convolution fusion | flops 116391936 | bytes 37748800 | tf_op jit(solution)/shard_map/qe,perfj->prfqj/dot_general | solution.py:53
  489.9 14.7 %copy.69 = bf16[9,2,64,1024]{2,1,0,3:T(2,128)(2,1)} copy(bf16[9,2,64,1024]{3,0,1,2:T(8,128)(2,1)} %convert_bitcast_fusion.1) | data formatting | bytes 4718592 | tf_op jit(solution)/shard_map/convert_element_type | solution.py:118
  523.0 18.4 %fusion.55 = (f32[1024,1024]{1,0:T(8,128)}, f32[1024,1024]{1,0:T(8,128)}) fusion(s32[1024,1024]{0,1:T(8,128)} %copy.56), kind=kLoop, calls=%fused_computation.65 | loop fusion | flops 13631488 | bytes 12582912 | tf_op jit(solution)/shard_map/sin | solution.py:14
  541.4 29.1 %all-to-all-done.1 = bf16[16,2,36864]{2,1,0:T(2,128)(2,1)S(1)} async-done(((bf16[16,2,36864]{2,1,0:T(2,128)(2,1)}), bf16[16,2,36864]{2,1,0:T(2,128)(2,1)S(1)}, u32[]{:S(2)}, u32[]{:S(2)}) %all-to-all-start.1) | async-done | bytes 2359328 | tf_op jit(solution)/shard_map/all_to_all | solution.py:117
  575.8 11.5 %copy.90 = bf16[9,2,64,16,64]{4,2,3,1,0:T(8,128)(2,1)} copy(bf16[9,2,64,16,64]{2,1,0,4,3:T(2,128)(2,1)} %bitcast.95) | data formatting | bytes 4718592 | tf_op jit(solution)/shard_map/all_to_all | solution.py:117
  587.2 166.2 %while.15 = (s32[]{:T(128)}, f32[1024,1024]{1,0:T(8,128)}, f32[1024,1024]{1,0:T(8,128)}, f32[9,64,2048]{2,1,0:T(8,128)}, f32[1024,1024]{1,0:T(8,128)}, /*index=5...) while((s32[]{:T(128)}, f32[1024,1024]{1,0:T(8,128)}, ...), condition=%wide.region_3.4_spmd.clone, body=%wide.region_2.3_spmd.clone.sunk | while | flops 584056832 | bytes 64225924 | solution.py:85
  608.9 10.6 %multiply_add_fusion.2 = (f32[1024,1024]{1,0:T(8,128)}, f32[1024,1024]{1,0:T(8,128)}) fusion(f32[1024,1024]{1,0:T(8,128)S(1)} %copy-done, f32[1024,1024]{1,0:T(8,128)} %get-tuple-element.196, f32[1024,1024]{1,0:T(8,128)} %get-tuple-element.185, f32[1024,1024]{1,0:T(8,128)} %get-tuple-element.184, pred[]{:T(512)S(6)} %compare.38), kind=kLoop, calls=%fused_computation.9.clone.1 | loop fusion | flops 8388608 | bytes 25165824 | tf_op jit(solution)/shard_map/while/body/eval_jaxpr/add | solution.py:81
  628.1 10.6 %multiply_add_fusion.2 = (f32[1024,1024]{1,0:T(8,128)}, f32[1024,1024]{1,0:T(8,128)}) fusion(f32[1024,1024]{1,0:T(8,128)S(1)} %copy-done, f32[1024,1024]{1,0:T(8,128)} %get-tuple-element.196, f32[1024,1024]{1,0:T(8,128)} %get-tuple-element.185, f32[1024,1024]{1,0:T(8,128)} %get-tuple-element.184, pred[]{:T(512)S(6)} %compare.38), kind=kLoop, calls=%fused_computation.9.clone.1 | loop fusion | flops 8388608 | bytes 25165824 | tf_op jit(solution)/shard_map/while/body/eval_jaxpr/add | solution.py:81
  647.2 10.6 %multiply_add_fusion.2 = (f32[1024,1024]{1,0:T(8,128)}, f32[1024,1024]{1,0:T(8,128)}) fusion(f32[1024,1024]{1,0:T(8,128)S(1)} %copy-done, f32[1024,1024]{1,0:T(8,128)} %get-tuple-element.196, f32[1024,1024]{1,0:T(8,128)} %get-tuple-element.185, f32[1024,1024]{1,0:T(8,128)} %get-tuple-element.184, pred[]{:T(512)S(6)} %compare.38), kind=kLoop, calls=%fused_computation.9.clone.1 | loop fusion | flops 8388608 | bytes 25165824 | tf_op jit(solution)/shard_map/while/body/eval_jaxpr/add | solution.py:81
  666.3 10.6 %multiply_add_fusion.2 = (f32[1024,1024]{1,0:T(8,128)}, f32[1024,1024]{1,0:T(8,128)}) fusion(f32[1024,1024]{1,0:T(8,128)S(1)} %copy-done, f32[1024,1024]{1,0:T(8,128)} %get-tuple-element.196, f32[1024,1024]{1,0:T(8,128)} %get-tuple-element.185, f32[1024,1024]{1,0:T(8,128)} %get-tuple-element.184, pred[]{:T(512)S(6)} %compare.38), kind=kLoop, calls=%fused_computation.9.clone.1 | loop fusion | flops 8388608 | bytes 25165824 | tf_op jit(solution)/shard_map/while/body/eval_jaxpr/add | solution.py:81
  685.4 10.6 %multiply_add_fusion.2 = (f32[1024,1024]{1,0:T(8,128)}, f32[1024,1024]{1,0:T(8,128)}) fusion(f32[1024,1024]{1,0:T(8,128)S(1)} %copy-done, f32[1024,1024]{1,0:T(8,128)} %get-tuple-element.196, f32[1024,1024]{1,0:T(8,128)} %get-tuple-element.185, f32[1024,1024]{1,0:T(8,128)} %get-tuple-element.184, pred[]{:T(512)S(6)} %compare.38), kind=kLoop, calls=%fused_computation.9.clone.1 | loop fusion | flops 8388608 | bytes 25165824 | tf_op jit(solution)/shard_map/while/body/eval_jaxpr/add | solution.py:81
  760.8 13.1 %fusion.48 = f32[64,16,1024]{2,1,0:T(8,128)} fusion(f32[9,64,2,1024]{3,2,1,0:T(2,128)} %reshape.315, f32[16,1,9]{2,0,1:T(8,128)S(1)} %get-tuple-element.114, f32[16,1,9]{2,0,1:T(8,128)S(1)} %get-tuple-element.113), kind=kOutput, calls=%fused_computation.60 | convolution fusion | flops 226492704 | bytes 8914048 | tf_op jit(solution)/shard_map/tuk,kbud->btd/dot_general | solution.py:97
  (92 shorter events, 192.9 us)
Async XLA Ops:
  0.0 34.1 %copy-start.6 = (bf16[128,16,2048]{2,1,0:T(8,128)(2,1)S(1)}, bf16[128,16,2048]{2,1,0:T(8,128)(2,1)}, u32[]{:S(2)}) copy-start(bf16[128,16,2048]{2,1,0:T(8,128)(2,1)} %param.7) | copy-start | bytes 25165828
  98.4 7.0 copy-start.5
  98.4 189.2 %all-to-all-start = ((bf16[128,16,2,1024]{0,1,2,3:T(8,128)(2,1)}), bf16[128,16,2,1024]{0,1,2,3:T(8,128)(2,1)}, u32[]{:S(2)}, u32[]{:S(2)}) async-start(bf16[128,16,2,1024]{0,1,2,3:T(8,128)(2,1)} %copy.58), calls=%async_computation | async-start | bytes 16777216 | tf_op jit(solution)/shard_map/all_to_all | solution.py:112
  375.4 6.5 copy-start.3
  381.9 37.2 %copy-start.1 = (f32[2,4,16,64,256]{4,3,2,1,0:T(8,128)}, f32[2,4,16,64,256]{4,3,2,1,0:T(8,128)S(1)}, u32[]{:S(2)}) copy-start(f32[2,4,16,64,256]{4,3,2,1,0:T(8,128)S(1)} %get-tuple-element.107) | copy-start | bytes 25165828
  382.0 18.8 %copy-start.4 = (f32[4,4,1,1,1]{1,0,4,3,2:T(4,128)S(1)}, f32[4,4,1,1,1]{1,0,4,3,2:T(4,128)}, u32[]{:S(2)}) copy-start(f32[4,4,1,1,1]{1,0,4,3,2:T(4,128)} %constant.123) | copy-start | bytes 196
  470.5 5.4 copy-start.2
  512.5 58.0 %all-to-all-start.1 = ((bf16[16,2,36864]{2,1,0:T(2,128)(2,1)}), bf16[16,2,36864]{2,1,0:T(2,128)(2,1)S(1)}, u32[]{:S(2)}, u32[]{:S(2)}) async-start(bf16[16,2,36864]{2,1,0:T(2,128)(2,1)} %reshape.334), calls=%async_computation.1 | async-start | bytes 4718592 | tf_op jit(solution)/shard_map/all_to_all | solution.py:117
  589.8 2.4 copy-start
  606.5 2.5 copy-start
  625.6 2.4 copy-start
  644.7 2.4 copy-start
  663.8 2.4 copy-start
  682.9 2.4 copy-start
  702.1 2.5 copy-start
  721.2 2.5 copy-start
  740.4 2.5 copy-start
where the time goes:
time: 784 us; the launch traced here: 774 us
  waiting for transfers between devices  209 us (27%)
  other arithmetic  201 us (26%)
  local copies, waits for them, and re-layouts  192 us (24%)
  matrix products  160 us (20%)
  starting transfers between devices  12.1 us (2%)
    all_to_all x1, waiting for transfers between devices, body(): lax.all_to_all(spectra, 'wide', split_axis=3, concat_axis=0, tiled=True)  180 us
    add x9, other arithmetic, one_term(): next_sin = sine * base_cos + cosine * base_sin  93.3 us
    gather x2, local copies, waits for them, and re-layouts, beam_power(): grid = jnp.take(spec, feed_index.reshape(-1), axis=0)  44.8 us
    neg x9, other arithmetic, one_term(): lower = jnp.concatenate([-sin_half, cos_half], axis=1)  41 us
    another operation x2, other arithmetic  34.1 us
    dot_general x1, matrix products, beam_power(): jnp.einsum('qe,perfj->prfqj', cosines, real_part, precision=high)  32.8 us
    reshape x2, local copies, waits for them, and re-layouts, body(): spectra = spectra.astype(jnp.bfloat16).reshape(feed_dev, frames, 2, nfreq)  31.3 us
    all_to_all x1, waiting for transfers between devices, body(): lax.all_to_all(local.astype(jnp.bfloat16), 'wide', split_axis=3, concat_a...  29.1 us
  transfers between devices with their start and end apart: 2, of which 2 were waited for; matrix products, arithmetic and copies ran while one was open for 3% of the time, Pallas kernels for 0%

commit v1 on v0

--- a/solution.py
+++ b/solution.py
@@ -7,6 +7,17 @@
 
 EAST_COSINE = np.array([[1, 1, 1, 1], [1, 0, -1, 0], [1, -1, 1, -1], [1, 0, -1, 0]], np.float32)
 EAST_SINE = np.array([[0, 0, 0, 0], [0, 1, 0, -1], [0, 0, 0, 0], [0, -1, 0, 1]], np.float32)
+
+
+def cut_along(x, dim, length):
+    before, after = (x.shape[:dim], x.shape[dim + 1 :])
+    return jnp.moveaxis(x.reshape(*before, length, -1, *after), dim, 0)
+
+
+def joined_along(pieces, dim):
+    pieces = jnp.moveaxis(pieces, 0, dim)
+    shape = pieces.shape
+    return pieces.reshape(*shape[:dim], shape[dim] * shape[dim + 1], *shape[dim + 2 :])
 
 
 def phase_pair(count, length):
@@ -114,9 +125,15 @@
     centred = (power - jnp.mean(power, axis=0, keepdims=True)).astype(jnp.bfloat16)
     time_table = transform_table(frames)
     local = jnp.einsum("okr,rfb->kofb", time_table, centred, preferred_element_type=jnp.float32)
-    spectrum = lax.all_to_all(
-        local.astype(jnp.bfloat16), "wide", split_axis=3, concat_axis=2, tiled=True
-    )
+    x = local.astype(jnp.bfloat16)
+    size, place = (lax.axis_size("wide"), lax.axis_index("wide"))
+    blocks = cut_along(x, 3, size)
+    outs = [blocks[place]]
+    for step in range(1, size):
+        sent = blocks[(place + step) % size]
+        outs.append(lax.ppermute(sent, "wide", [(i, (i + step) % size) for i in range(size)]))
+    blocks = jnp.stack(outs)[(place - jnp.arange(size)) % size]
+    spectrum = joined_along(blocks, 2)
     trials = dedisperse(spectrum, dm_delay, frames)
     return synthesis(trials, frames, nfreq)
 

time: 784 us -> 839 us (1.070)
  waiting for transfers between devices: 209 us -> 248 us
  local copies, waits for them, and re-layouts: 192 us -> 204 us
    ppermute x0 -> x15, waiting for transfers between devices: none -> 92.8 us  [body(): lax.ppermute(sent, 'wide', [(i, (i + step) % size) for i in range(size)])]
    all_to_all x1 -> x0, waiting for transfers between devices: 29.1 us -> none  [body(): lax.all_to_all(local.astype(jnp.bfloat16), 'wide', split_axis=3, concat_a...]
    all_to_all x1, waiting for transfers between devices: 180 us -> 155 us  [body(): lax.all_to_all(spectra, 'wide', split_axis=3, concat_axis=0, tiled=True)]
    another operation x0 -> x2, local copies, waits for them, and re-layouts: none -> 21.9 us
    convert_element_type x1, local copies, waits for them, and re-layouts: 14.7 us -> 1.43 us  [body(): x = local.astype(jnp.bfloat16)]
    all_to_all x1 -> x0, local copies, waits for them, and re-layouts: 11.5 us -> none  [body(): lax.all_to_all(local.astype(jnp.bfloat16), 'wide', split_axis=3, concat_a...]
    unnamed x16 -> x49, local copies, waits for them, and re-layouts: 18.5 us -> 23.3 us
  transfers between devices with their start and end apart: 2 -> 16, of which waited for: 2 -> 11; matrix products, arithmetic and copies ran while one was open for 3% -> 5% of each run, Pallas kernels for 0% -> 0%
where the time goes in v1:
time: 839 us; the launch traced here: 828 us
  waiting for transfers between devices  248 us (30%)
  local copies, waits for them, and re-layouts  204 us (24%)
  other arithmetic  202 us (24%)
  matrix products  157 us (19%)
  starting transfers between devices  15.6 us (2%)
    all_to_all x1, waiting for transfers between devices, body(): lax.all_to_all(spectra, 'wide', split_axis=3, concat_axis=0, tiled=True)  155 us
    add x9, other arithmetic, one_term(): next_sin = sine * base_cos + cosine * base_sin  93.3 us
    ppermute x15, waiting for transfers between devices, body(): lax.ppermute(sent, 'wide', [(i, (i + step) % size) for i in range(size)])  92.8 us
    gather x2, local copies, waits for them, and re-layouts, beam_power(): grid = jnp.take(spec, feed_index.reshape(-1), axis=0)  44.7 us
    neg x9, other arithmetic, one_term(): lower = jnp.concatenate([-sin_half, cos_half], axis=1)  41 us
    another operation x2, other arithmetic  34.1 us
    dot_general x1, matrix products, beam_power(): jnp.einsum('qe,perfj->prfqj', cosines, real_part, precision=high)  33 us
    reshape x2, local copies, waits for them, and re-layouts, body(): spectra = spectra.astype(jnp.bfloat16).reshape(feed_dev, frames, 2, nfreq)  31.4 us
  transfers between devices with their start and end apart: 16, of which 11 were waited for; matrix products, arithmetic and copies ran while one was open for 5% of the time, Pallas kernels for 0%

profile of v1, /device:TPU:13, one launch (start us, length us, event | category | flops | bytes accessed | tf_op | source)
XLA Modules:
  0.0 827.9 jit_solution(17816016748847486865)
XLA Ops:
  0.0 34.1 %multiply_convert_fusion = (bf16[2048,1024]{1,0:T(8,128)(2,1)S(1)}, bf16[2048,1024]{1,0:T(8,128)(2,1)S(1)}) fusion(), kind=kLoop, calls=%fused_computation.37 | loop fusion | flops 39845888 | bytes 8388608 | tf_op jit(solution)/shard_map/convert.3
  34.1 20.6 %convert_bitcast_fusion = bf16[2048,2048]{0,1:T(8,128)(2,1)} fusion(bf16[2048,2048]{1,0:T(8,128)(2,1)S(1)} %bitcast.190, bf16[2048,1024]{1,0:T(8,128)(2,1)S(1)} %get-tuple-element.131, bf16[2048,1024]{1,0:T(8,128)(2,1)S(1)} %get-tuple-element.132), kind=kOutput, calls=%fused_computation.36 | convolution fusion | flops 17200840704 | bytes 25165824 | tf_op jit(solution)/shard_map/dot_general | solution.py:115
  54.7 12.3 %copy.55 = bf16[2048,2048]{1,0:T(8,128)(2,1)} copy(bf16[2048,2048]{0,1:T(8,128)(2,1)} %convert_bitcast_fusion) | data formatting | bytes 16777216 | tf_op jit(solution)/shard_map/convert_element_type | solution.py:118
  67.0 14.5 %reshape.400 = bf16[128,16,2,1024]{3,2,1,0:T(2,128)(2,1)} reshape(bf16[2048,2048]{1,0:T(8,128)(2,1)} %copy.55) | data formatting | bytes 16777216 | tf_op jit(solution)/shard_map/reshape | solution.py:118
  81.6 16.9 %copy.56 = bf16[128,16,2,1024]{0,1,2,3:T(8,128)(2,1)} copy(bf16[128,16,2,1024]{3,2,1,0:T(2,128)(2,1)} %reshape.400) | data formatting | bytes 16777216 | tf_op jit(solution)/shard_map/reshape | solution.py:118
  114.3 18.4 %fusion.55 = (f32[1024,1024]{1,0:T(8,128)}, f32[1024,1024]{1,0:T(8,128)}) fusion(s32[1024,1024]{0,1:T(8,128)} %copy.54), kind=kLoop, calls=%fused_computation.66 | loop fusion | flops 13631488 | bytes 12582912 | tf_op jit(solution)/shard_map/sin | solution.py:25
  132.7 155.2 %all-to-all-done = bf16[128,16,2,1024]{0,1,2,3:T(8,128)(2,1)} async-done(((bf16[128,16,2,1024]{0,1,2,3:T(8,128)(2,1)}), bf16[128,16,2,1024]{0,1,2,3:T(8,128)(2,1)}, u32[]{:S(2)}, u32[]{:S(2)}) %all-to-all-start) | async-done | bytes 8388640 | tf_op jit(solution)/shard_map/all_to_all | solution.py:123
  287.9 29.1 %copy.79 = bf16[16,128,16,2,64]{4,2,3,1,0:T(8,128)(2,1)} copy(bf16[16,128,16,2,64]{1,2,3,4,0:T(8,128)(2,1)} %bitcast.5) | data formatting | bytes 16777216 | tf_op jit(solution)/shard_map/all_to_all | solution.py:123
  317.0 25.0 %gather_fusion = bf16[2048,16,2,64]{3,1,2,0:T(8,128)(2,1)} fusion(bf16[2048,16,2,64]{3,1,2,0:T(8,128)(2,1)} %bitcast.167, s32[2048]{0:T(1024)S(1)} %broadcast_clamp_fusion), kind=kCustom, calls=%fused_computation | custom fusion | bytes 16785408 | tf_op jit(solution)/shard_map/jit(_take)/gather | solution.py:55
  342.0 19.7 %copy.80 = bf16[2,4,256,16,2,64]{2,1,0,5,4,3:T(4,128)(2,1)} copy(bf16[2,4,256,16,2,64]{5,3,4,2,1,0:T(8,128)(2,1)} %bitcast.168) | data formatting | bytes 16777216 | tf_op jit(solution)/shard_map/jit(_take)/gather | solution.py:55
  382.2 18.6 %fusion.31 = f32[2,16,64,256,4]{3,4,2,1,0:T(4,128)} fusion(f32[4,4,1,1,1]{1,0,4,3,2:T(4,128)S(1)} %copy-done.5, f32[2,4,16,64,256]{4,3,2,1,0:T(8,128)S(1)} %get-tuple-element.108), kind=kOutput, calls=%fused_computation.42 | convolution fusion | flops 100663296 | bytes 16777280 | tf_op jit(solution)/shard_map/qe,perfj->prfqj/dot_general | solution.py:68
  400.8 18.4 %fusion.33 = f32[2,16,64,256,4]{3,4,2,1,0:T(4,128)} fusion(f32[4,4,1,1,1]{1,0,4,3,2:T(4,128)S(1)} %copy-done.6, f32[2,4,16,64,256]{4,3,2,1,0:T(8,128)S(1)} %get-tuple-element.108), kind=kOutput, calls=%fused_computation.44 | convolution fusion | flops 100663296 | bytes 16777280 | tf_op jit(solution)/shard_map/qe,perfj->prfqj/dot_general | solution.py:65
  419.2 18.5 %fusion.35 = f32[2,16,64,256,4]{3,4,2,1,0:T(4,128)} fusion(f32[4,4,1,1,1]{1,0,4,3,2:T(4,128)S(1)} %copy-done.6, f32[2,4,16,64,256]{4,3,2,1,0:T(8,128)S(1)} %get-tuple-element.107), kind=kOutput, calls=%fused_computation.46 | convolution fusion | flops 100663296 | bytes 16777280 | tf_op jit(solution)/shard_map/qe,perfj->prfqj/dot_general | solution.py:69
  437.8 33.0 %add_reduce_fusion = f32[16,64,256,4]{2,3,1,0:T(4,128)} fusion(f32[2,16,64,256,4]{3,4,2,1,0:T(4,128)} %fusion.31, f32[2,16,64,256,4]{3,4,2,1,0:T(4,128)} %fusion.35, f32[2,16,64,256,4]{3,4,2,1,0:T(4,128)} %fusion.33, f32[4,4,1,1,1]{1,0,4,3,2:T(4,128)S(1)} %copy-done.5, f32[2,4,16,64,256]{4,3,2,1,0:T(8,128)} %copy-done.1), kind=kOutput, calls=%fused_computation.34 | convolution fusion | flops 116391936 | bytes 37748800 | tf_op jit(solution)/shard_map/qe,perfj->prfqj/dot_general | solution.py:64
  494.3 21.1 %constant_dynamic-slice_fusion.1 = (bf16[9,2,64,1,64]{4,3,2,1,0:T(2,128)(2,1)S(1)}, bf16[9,2,64,1,64]{4,3,2,1,0:T(2,128)(2,1)S(1)}, bf16[9,2,64,1,64]{4,3,2,1,0:...) fusion(bf16[9,2,64,16,64]{4,3,2,1,0:T(8,128)(2,1)} %reshape.401, ...), kind=kLoop, calls=%fused_computation.150 | loop fusion | bytes 4718656 | tf_op jit(solution)/shard_map/dynamic-slice.15
  536.8 34.0 %collective-permute-done.3 = bf16[9,2,64,64]{3,2,1,0:T(8,128)(2,1)S(1)} collective-permute-done((bf16[9,2,64,64]{3,2,1,0:T(8,128)(2,1)S(1)}, bf16[9,2,64,64]{3,2,1,0:T(8,128)(2,1)S(1)}, u32[]{:S(2)}, u32[]{:S(2)}) %collective-permute-start.3) | collective-permute-done | bytes 147488 | tf_op jit(solution)/shard_map/ppermute | solution.py:134
  571.5 15.1 %collective-permute-done.4 = bf16[9,2,64,64]{3,2,1,0:T(8,128)(2,1)S(1)} collective-permute-done((bf16[9,2,64,64]{3,2,1,0:T(8,128)(2,1)S(1)}, bf16[9,2,64,64]{3,2,1,0:T(8,128)(2,1)S(1)}, u32[]{:S(2)}, u32[]{:S(2)}) %collective-permute-start.4) | collective-permute-done | bytes 147488 | tf_op jit(solution)/shard_map/ppermute | solution.py:134
  593.8 11.7 %collective-permute-done.6 = bf16[9,2,64,64]{3,2,1,0:T(8,128)(2,1)S(1)} collective-permute-done((bf16[9,2,64,64]{3,2,1,0:T(8,128)(2,1)S(1)}, bf16[9,2,64,64]{3,2,1,0:T(8,128)(2,1)S(1)}, u32[]{:S(2)}, u32[]{:S(2)}) %collective-permute-start.6) | collective-permute-done | bytes 147488 | tf_op jit(solution)/shard_map/ppermute | solution.py:134
  641.1 166.3 %while.15 = (s32[]{:T(128)}, f32[1024,1024]{1,0:T(8,128)}, f32[1024,1024]{1,0:T(8,128)}, f32[9,64,2048]{2,1,0:T(8,128)}, f32[1024,1024]{1,0:T(8,128)}, /*index=5...) while((s32[]{:T(128)}, f32[1024,1024]{1,0:T(8,128)}, ...), condition=%wide.region_3.4_spmd.clone, body=%wide.region_2.3_spmd.clone.sunk | while | flops 584056832 | bytes 64225924 | solution.py:96
  663.0 10.6 %multiply_add_fusion.2 = (f32[1024,1024]{1,0:T(8,128)}, f32[1024,1024]{1,0:T(8,128)}) fusion(f32[1024,1024]{1,0:T(8,128)S(1)} %copy-done, f32[1024,1024]{1,0:T(8,128)} %get-tuple-element.212, f32[1024,1024]{1,0:T(8,128)} %get-tuple-element.201, f32[1024,1024]{1,0:T(8,128)} %get-tuple-element.200, pred[]{:T(512)S(6)} %compare.60), kind=kLoop, calls=%fused_computation.10.clone.1 | loop fusion | flops 8388608 | bytes 25165824 | tf_op jit(solution)/shard_map/while/body/eval_jaxpr/add | solution.py:92
  682.1 10.6 %multiply_add_fusion.2 = (f32[1024,1024]{1,0:T(8,128)}, f32[1024,1024]{1,0:T(8,128)}) fusion(f32[1024,1024]{1,0:T(8,128)S(1)} %copy-done, f32[1024,1024]{1,0:T(8,128)} %get-tuple-element.212, f32[1024,1024]{1,0:T(8,128)} %get-tuple-element.201, f32[1024,1024]{1,0:T(8,128)} %get-tuple-element.200, pred[]{:T(512)S(6)} %compare.60), kind=kLoop, calls=%fused_computation.10.clone.1 | loop fusion | flops 8388608 | bytes 25165824 | tf_op jit(solution)/shard_map/while/body/eval_jaxpr/add | solution.py:92
  701.2 10.6 %multiply_add_fusion.2 = (f32[1024,1024]{1,0:T(8,128)}, f32[1024,1024]{1,0:T(8,128)}) fusion(f32[1024,1024]{1,0:T(8,128)S(1)} %copy-done, f32[1024,1024]{1,0:T(8,128)} %get-tuple-element.212, f32[1024,1024]{1,0:T(8,128)} %get-tuple-element.201, f32[1024,1024]{1,0:T(8,128)} %get-tuple-element.200, pred[]{:T(512)S(6)} %compare.60), kind=kLoop, calls=%fused_computation.10.clone.1 | loop fusion | flops 8388608 | bytes 25165824 | tf_op jit(solution)/shard_map/while/body/eval_jaxpr/add | solution.py:92
  720.3 10.6 %multiply_add_fusion.2 = (f32[1024,1024]{1,0:T(8,128)}, f32[1024,1024]{1,0:T(8,128)}) fusion(f32[1024,1024]{1,0:T(8,128)S(1)} %copy-done, f32[1024,1024]{1,0:T(8,128)} %get-tuple-element.212, f32[1024,1024]{1,0:T(8,128)} %get-tuple-element.201, f32[1024,1024]{1,0:T(8,128)} %get-tuple-element.200, pred[]{:T(512)S(6)} %compare.60), kind=kLoop, calls=%fused_computation.10.clone.1 | loop fusion | flops 8388608 | bytes 25165824 | tf_op jit(solution)/shard_map/while/body/eval_jaxpr/add | solution.py:92
  814.8 12.9 %fusion.48 = f32[64,16,1024]{2,1,0:T(8,128)} fusion(f32[9,64,2,1024]{3,2,1,0:T(2,128)} %reshape.403, f32[16,1,9]{2,0,1:T(8,128)S(1)} %copy-done.4, f32[16,1,9]{2,0,1:T(8,128)S(1)} %copy-done.3), kind=kOutput, calls=%fused_computation.61 | convolution fusion | flops 226492704 | bytes 8914048 | tf_op jit(solution)/shard_map/tuk,kbud->btd/dot_general | solution.py:108
  (158 shorter events, 255.0 us)
Async XLA Ops:
  0.0 34.1 %copy-start.8 = (bf16[128,16,2048]{2,1,0:T(8,128)(2,1)S(1)}, bf16[128,16,2048]{2,1,0:T(8,128)(2,1)}, u32[]{:S(2)}) copy-start(bf16[128,16,2048]{2,1,0:T(8,128)(2,1)} %param.7) | copy-start | bytes 25165828
  98.4 7.5 copy-start.7
  98.4 189.5 %all-to-all-start = ((bf16[128,16,2,1024]{0,1,2,3:T(8,128)(2,1)}), bf16[128,16,2,1024]{0,1,2,3:T(8,128)(2,1)}, u32[]{:S(2)}, u32[]{:S(2)}) async-start(bf16[128,16,2,1024]{0,1,2,3:T(8,128)(2,1)} %copy.56), calls=%async_computation | async-start | bytes 16777216 | tf_op jit(solution)/shard_map/all_to_all | solution.py:123
  375.6 6.5 copy-start.5
  382.2 37.1 %copy-start.1 = (f32[2,4,16,64,256]{4,3,2,1,0:T(8,128)}, f32[2,4,16,64,256]{4,3,2,1,0:T(8,128)S(1)}, u32[]{:S(2)}) copy-start(f32[2,4,16,64,256]{4,3,2,1,0:T(8,128)S(1)} %get-tuple-element.107) | copy-start | bytes 25165828
  382.2 18.6 %copy-start.6 = (f32[4,4,1,1,1]{1,0,4,3,2:T(4,128)S(1)}, f32[4,4,1,1,1]{1,0,4,3,2:T(4,128)}, u32[]{:S(2)}) copy-start(f32[4,4,1,1,1]{1,0,4,3,2:T(4,128)} %constant.227) | copy-start | bytes 196
  470.7 5.5 copy-start.2
  515.5 8.3 collective-permute-start
  517.3 12.5 %collective-permute-start.1 = (bf16[9,2,64,64]{3,2,1,0:T(8,128)(2,1)S(1)}, bf16[9,2,64,64]{3,2,1,0:T(8,128)(2,1)S(1)}, u32[]{:S(2)}, u32[]{:S(2)}) collective-permute-start(bf16[9,2,64,64]{3,2,1,0:T(8,128)(2,1)S(1)} %bitcast.187), channel_id=1, source_target_pairs={{0,2},{1,3},{2,4},{3,5},{4,6},{5,7},{6,8},{7,9},{8,10},{9,11},{10,... | collective-permute-start | bytes 442376 | tf_op jit(solution)/shard_map/ppermute | solution.py:134
  517.4 18.6 %collective-permute-start.2 = (bf16[9,2,64,64]{3,2,1,0:T(8,128)(2,1)S(1)}, bf16[9,2,64,64]{3,2,1,0:T(8,128)(2,1)S(1)}, u32[]{:S(2)}, u32[]{:S(2)}) collective-permute-start(bf16[9,2,64,64]{3,2,1,0:T(8,128)(2,1)S(1)} %bitcast.186), channel_id=1, source_target_pairs={{0,3},{1,4},{2,5},{3,6},{4,7},{5,8},{6,9},{7,10},{8,11},{9,12},{10... | collective-permute-start | bytes 442376 | tf_op jit(solution)/shard_map/ppermute | solution.py:134
  517.5 53.2 %collective-permute-start.3 = (bf16[9,2,64,64]{3,2,1,0:T(8,128)(2,1)S(1)}, bf16[9,2,64,64]{3,2,1,0:T(8,128)(2,1)S(1)}, u32[]{:S(2)}, u32[]{:S(2)}) collective-permute-start(bf16[9,2,64,64]{3,2,1,0:T(8,128)(2,1)S(1)} %bitcast.185), channel_id=1, source_target_pairs={{0,4},{1,5},{2,6},{3,7},{4,8},{5,9},{6,10},{7,11},{8,12},{9,13},{1... | collective-permute-start | bytes 442376 | tf_op jit(solution)/shard_map/ppermute | solution.py:134
  518.5 68.1 %collective-permute-start.4 = (bf16[9,2,64,64]{3,2,1,0:T(8,128)(2,1)S(1)}, bf16[9,2,64,64]{3,2,1,0:T(8,128)(2,1)S(1)}, u32[]{:S(2)}, u32[]{:S(2)}) collective-permute-start(bf16[9,2,64,64]{3,2,1,0:T(8,128)(2,1)S(1)} %bitcast.184), channel_id=1, source_target_pairs={{0,5},{1,6},{2,7},{3,8},{4,9},{5,10},{6,11},{7,12},{8,13},{9,14},{... | collective-permute-start | bytes 442376 | tf_op jit(solution)/shard_map/ppermute | solution.py:134
  523.8 69.1 %collective-permute-start.5 = (bf16[9,2,64,64]{3,2,1,0:T(8,128)(2,1)S(1)}, bf16[9,2,64,64]{3,2,1,0:T(8,128)(2,1)S(1)}, u32[]{:S(2)}, u32[]{:S(2)}) collective-permute-start(bf16[9,2,64,64]{3,2,1,0:T(8,128)(2,1)S(1)} %bitcast.183), channel_id=1, source_target_pairs={{0,6},{1,7},{2,8},{3,9},{4,10},{5,11},{6,12},{7,13},{8,14},{9,15},... | collective-permute-start | bytes 442376 | tf_op jit(solution)/shard_map/ppermute | solution.py:134
  529.8 75.7 %collective-permute-start.6 = (bf16[9,2,64,64]{3,2,1,0:T(8,128)(2,1)S(1)}, bf16[9,2,64,64]{3,2,1,0:T(8,128)(2,1)S(1)}, u32[]{:S(2)}, u32[]{:S(2)}) collective-permute-start(bf16[9,2,64,64]{3,2,1,0:T(8,128)(2,1)S(1)} %bitcast.182), channel_id=1, source_target_pairs={{0,7},{1,8},{2,9},{3,10},{4,11},{5,12},{6,13},{7,14},{8,15},{9,0},... | collective-permute-start | bytes 442376 | tf_op jit(solution)/shard_map/ppermute | solution.py:134
  536.0 79.0 %collective-permute-start.7 = (bf16[9,2,64,64]{3,2,1,0:T(8,128)(2,1)S(1)}, bf16[9,2,64,64]{3,2,1,0:T(8,128)(2,1)S(1)}, u32[]{:S(2)}, u32[]{:S(2)}) collective-permute-start(bf16[9,2,64,64]{3,2,1,0:T(8,128)(2,1)S(1)} %bitcast.181), channel_id=1, source_target_pairs={{0,8},{1,9},{2,10},{3,11},{4,12},{5,13},{6,14},{7,15},{8,0},{9,1},... | collective-permute-start | bytes 442376 | tf_op jit(solution)/shard_map/ppermute | solution.py:134
  570.8 45.0 %collective-permute-start.8 = (bf16[9,2,64,64]{3,2,1,0:T(8,128)(2,1)S(1)}, bf16[9,2,64,64]{3,2,1,0:T(8,128)(2,1)S(1)}, u32[]{:S(2)}, u32[]{:S(2)}) collective-permute-start(bf16[9,2,64,64]{3,2,1,0:T(8,128)(2,1)S(1)} %bitcast.180), channel_id=1, source_target_pairs={{0,9},{1,10},{2,11},{3,12},{4,13},{5,14},{6,15},{7,0},{8,1},{9,2},... | collective-permute-start | bytes 442376 | tf_op jit(solution)/shard_map/ppermute | solution.py:134
  586.6 30.0 %collective-permute-start.9 = (bf16[9,2,64,64]{3,2,1,0:T(8,128)(2,1)S(1)}, bf16[9,2,64,64]{3,2,1,0:T(8,128)(2,1)S(1)}, u32[]{:S(2)}, u32[]{:S(2)}) collective-permute-start(bf16[9,2,64,64]{3,2,1,0:T(8,128)(2,1)S(1)} %bitcast.179), channel_id=1, source_target_pairs={{0,10},{1,11},{2,12},{3,13},{4,14},{5,15},{6,0},{7,1},{8,2},{9,3},... | collective-permute-start | bytes 442376 | tf_op jit(solution)/shard_map/ppermute | solution.py:134
  592.9 24.7 %collective-permute-start.10 = (bf16[9,2,64,64]{3,2,1,0:T(8,128)(2,1)S(1)}, bf16[9,2,64,64]{3,2,1,0:T(8,128)(2,1)S(1)}, u32[]{:S(2)}, u32[]{:S(2)}) collective-permute-start(bf16[9,2,64,64]{3,2,1,0:T(8,128)(2,1)S(1)} %bitcast.178), channel_id=1, source_target_pairs={{0,11},{1,12},{2,13},{3,14},{4,15},{5,0},{6,1},{7,2},{8,3},{9,4},{... | collective-permute-start | bytes 442376 | tf_op jit(solution)/shard_map/ppermute | solution.py:134
  605.5 12.8 %collective-permute-start.11 = (bf16[9,2,64,64]{3,2,1,0:T(8,128)(2,1)S(1)}, bf16[9,2,64,64]{3,2,1,0:T(8,128)(2,1)S(1)}, u32[]{:S(2)}, u32[]{:S(2)}) collective-permute-start(bf16[9,2,64,64]{3,2,1,0:T(8,128)(2,1)S(1)} %bitcast.177), channel_id=1, source_target_pairs={{0,12},{1,13},{2,14},{3,15},{4,0},{5,1},{6,2},{7,3},{8,4},{9,5},{1... | collective-permute-start | bytes 442376 | tf_op jit(solution)/shard_map/ppermute | solution.py:134
  615.0 6.4 collective-permute-start.12
  615.8 11.1 %collective-permute-start.13 = (bf16[9,2,64,64]{3,2,1,0:T(8,128)(2,1)S(1)}, bf16[9,2,64,64]{3,2,1,0:T(8,128)(2,1)S(1)}, u32[]{:S(2)}, u32[]{:S(2)}) collective-permute-start(bf16[9,2,64,64]{3,2,1,0:T(8,128)(2,1)S(1)} %bitcast.175), channel_id=1, source_target_pairs={{0,14},{1,15},{2,0},{3,1},{4,2},{5,3},{6,4},{7,5},{8,6},{9,7},{10,... | collective-permute-start | bytes 442376 | tf_op jit(solution)/shard_map/ppermute | solution.py:134
  616.5 12.0 %collective-permute-start.14 = (bf16[9,2,64,64]{3,2,1,0:T(8,128)(2,1)S(1)}, bf16[9,2,64,64]{3,2,1,0:T(8,128)(2,1)S(1)}, u32[]{:S(2)}, u32[]{:S(2)}) collective-permute-start(bf16[9,2,64,64]{3,2,1,0:T(8,128)(2,1)S(1)} %bitcast.174), channel_id=1, source_target_pairs={{0,15},{1,0},{2,1},{3,2},{4,3},{5,4},{6,5},{7,6},{8,7},{9,8},{10,9... | collective-permute-start | bytes 442376 | tf_op jit(solution)/shard_map/ppermute | solution.py:134
  807.4 7.4 copy-start.3
  807.4 7.4 copy-start.4
  (9 other events, 22.0 us)
